TPU v7x, 256 devices: a whole 4x4x8 slice. The times are simulated.
256 devices in a mesh: lat: 16 (over z_lo, x, core), lon: 4 (over y), bin: 4 (over z_hi).
Axes of the slice: x: 4, y: 4, z: 8 (z_hi: 4, z_lo: 2; z = z_hi * 2 + z_lo), core: 2. Of those that a mesh axis runs over, the one named last changes fastest.
Arguments:
- inputs: bfloat16 [512, 1024, 128], P(('lat', 'bin'), 'lon'), may hold values from -70 to 70
- conv_one: bfloat16 [3, 3, 128, 128], replicated, may hold values from -0.1875 to 0.1875
- conv_two: bfloat16 [3, 3, 128, 128], replicated, may hold values from -0.1875 to 0.1875
- head_weight: bfloat16 [4, 128, 512], P(None, None, 'bin'), may hold values from -45.078057 to 45.078057
- targets: int32 [4, 512, 1024], P(None, 'lat', 'lon'), may hold values from 0 to 511
Outputs:
- loss_mean: float32 [], replicated
- grad_conv_one: float32 [3, 3, 128, 128], replicated
- grad_conv_two: float32 [3, 3, 128, 128], replicated
- grad_heads: float32 [4, 128, 512], P(None, None, 'bin')
All inputs are finite; a program needn't handle non-finite values.
Results may differ from a plain program's by a relative error of at most 0.0035.
The roundings to bfloat16 on the way count: a program that leaves them out, or rounds other values in their place, can miss the bound.
Values may be sent and summed in bfloat16 or wider, within the bound.
A program may use at most 64 MiB of HBM per device.

v0:
```python
import math
import jax
import jax.numpy as jnp
from jax import lax
from jax.sharding import PartitionSpec as P


def extended(shard, sides, width):
    for axis, dim in sides:
        devices, length = (lax.axis_size(axis), shard.shape[dim])
        up = [(i, (i + 1) % devices) for i in range(devices - 1)]
        down = [(j, i) for i, j in up]
        last = lax.slice_in_dim(shard, length - width, length, axis=dim)
        leading = lax.slice_in_dim(shard, 0, width, axis=dim)
        before = lax.ppermute(last, axis, up)
        after = lax.ppermute(leading, axis, down)
        shard = jnp.concatenate([before, shard, after], axis=dim)
    return shard


def merged(shard, axis, combine):
    everything = jax.tree.map(lambda part: lax.all_gather(part, axis), shard)
    leading = jax.tree.map(lambda part: part[0], everything)

    def lap(k, so_far):
        return combine(so_far, jax.tree.map(lambda part: part[k], everything))

    return lax.fori_loop(1, lax.axis_size(axis), lap, leading)


def patches(padded, grid_rows, grid_cols):
    slices = [padded[a : a + grid_rows, b : b + grid_cols] for a in range(3) for b in range(3)]
    return jnp.concatenate(slices, axis=2).reshape(grid_rows * grid_cols, -1)


def rimmed(values_in):
    return extended(values_in, ((("lat", "bin"), 0), ("lon", 1)), 1)


def softmax_join(left, right):
    highest = jnp.maximum(left[0], right[0])
    summed = left[1] * jnp.exp(left[0] - highest) + right[1] * jnp.exp(right[0] - highest)
    return (highest, summed, left[2] + right[2])


def per_device(inputs, conv_one, conv_two, head_weight, targets):
    grid_rows, grid_cols, channels = inputs.shape
    head_count = head_weight.shape[0]
    cells_all = (
        grid_rows * lax.axis_size("lat") * lax.axis_size("bin") * grid_cols * lax.axis_size("lon")
    )
    loss_scale = 1.0 / math.sqrt(head_count * cells_all)
    inner_one = patches(rimmed(inputs), grid_rows, grid_cols)
    pre_one = jnp.dot(
        inner_one, conv_one.reshape(9 * channels, channels), preferred_element_type=jnp.float32
    )
    act_one = jnp.maximum(pre_one, 0.0).astype(jnp.bfloat16)
    inner_two = patches(
        rimmed(act_one.reshape(grid_rows, grid_cols, channels)), grid_rows, grid_cols
    )
    pre_two = jnp.dot(
        inner_two, conv_two.reshape(9 * channels, channels), preferred_element_type=jnp.float32
    )
    act_two = jnp.maximum(pre_two, 0.0).astype(jnp.bfloat16)
    gathered = lax.all_gather(
        act_two.reshape(grid_rows, grid_cols, channels), "bin", axis=0, tiled=True
    )
    features = gathered.reshape(-1, channels)
    labels = targets.reshape(head_count, -1)
    first_bin = lax.axis_index("bin") * head_weight.shape[2]
    cell_count = features.shape[0]
    bin_width = head_weight.shape[2]
    block_rows = math.gcd(cell_count, 1024)
    block_count = cell_count // block_rows
    feat_blocks = features.reshape(block_count, block_rows, channels)
    label_blocks = labels.reshape(head_count, block_count, block_rows).transpose(1, 0, 2)
    columns = jnp.arange(bin_width, dtype=jnp.int32)[None, :] + first_bin

    def head_stats(inputs_now):
        feat_rows, label_rows = inputs_now
        maxima, totals, picked = ([], [], [])
        for k in range(head_count):
            logits = jnp.dot(feat_rows, head_weight[k], preferred_element_type=jnp.float32)
            highest = jnp.max(logits, axis=1)
            maxima.append(highest)
            totals.append(jnp.sum(jnp.exp(logits - highest[:, None]), axis=1))
            picked.append(
                jnp.sum(jnp.where(columns == label_rows[k][:, None], logits, 0.0), axis=1)
            )
        return (jnp.stack(maxima), jnp.stack(totals), jnp.stack(picked))

    maxima, totals, picked = lax.map(head_stats, (feat_blocks, label_blocks))
    maxima, totals, picked = merged((maxima, totals, picked), "bin", softmax_join)
    log_total = maxima + jnp.log(totals)
    loss_part = jnp.sum(log_total - picked)

    def backward(gradients, inputs_now):
        feat_rows, label_rows, total_rows = inputs_now
        hidden_back = jnp.zeros((block_rows, channels), jnp.float32)
        for k in range(head_count):
            logits = jnp.dot(feat_rows, head_weight[k], preferred_element_type=jnp.float32)
            chosen = columns == label_rows[k][:, None]
            logit_grad = (
                (jnp.exp(logits - total_rows[k][:, None]) - jnp.where(chosen, 1.0, 0.0))
                * loss_scale
            ).astype(jnp.bfloat16)
            gradients = gradients.at[k].add(
                jnp.einsum("nc,nv->cv", feat_rows, logit_grad, preferred_element_type=jnp.float32)
            )
            hidden_back = hidden_back + jnp.einsum(
                "nv,cv->nc", logit_grad, head_weight[k], preferred_element_type=jnp.float32
            )
        return (gradients, hidden_back)

    start = jnp.zeros((head_count, channels, bin_width), jnp.float32)
    head_grads, backs = lax.scan(backward, start, (feat_blocks, label_blocks, log_total))
    hidden_back = backs.reshape(cell_count, channels)
    hidden_back = lax.psum_scatter(hidden_back, "bin", scatter_dimension=0, tiled=True)
    back_two = jnp.where(pre_two > 0, hidden_back, 0.0).astype(jnp.bfloat16)
    grad_two = jnp.einsum("nk,nc->kc", inner_two, back_two, preferred_element_type=jnp.float32)
    flipped = conv_two[::-1, ::-1].transpose(0, 1, 3, 2).reshape(9 * channels, channels)
    outer_two = patches(
        rimmed(back_two.reshape(grid_rows, grid_cols, channels)), grid_rows, grid_cols
    )
    back_act = jnp.dot(outer_two, flipped, preferred_element_type=jnp.float32)
    back_one = jnp.where(pre_one > 0, back_act, 0.0).astype(jnp.bfloat16)
    grad_one = jnp.einsum("nk,nc->kc", inner_one, back_one, preferred_element_type=jnp.float32)
    grad_one, grad_two = lax.psum((grad_one, grad_two), ("lat", "lon", "bin"))
    head_grads, loss_sum = lax.psum((head_grads, loss_part), ("lat", "lon"))
    loss_mean = loss_sum / (head_count * cells_all)
    grad_conv_one = grad_one.reshape(3, 3, channels, channels)
    grad_conv_two = grad_two.reshape(3, 3, channels, channels)
    return (loss_mean, grad_conv_one, grad_conv_two, head_grads)


def solution(mesh):
    in_specs = (
        P(("lat", "bin"), "lon", None),
        P(),
        P(),
        P(None, None, "bin"),
        P(None, "lat", "lon"),
    )
    out_specs = (P(), P(), P(), P(None, None, "bin"))
    return jax.shard_map(
        per_device, mesh=mesh, in_specs=in_specs, out_specs=out_specs, check_vma=False
    )
```

profile of v0, /device:TPU:8, one launch (start us, length us, event | category | flops | bytes accessed | tf_op | source)
XLA Modules:
  0.0 1140.5 jit_solution(2076384683649284297)
XLA Ops:
  8.2 5.2 collective-permute-start
  13.4 1.3 collective-permute-start.1
  16.4 6.6 collective-permute-done.1
  23.0 3.5 collective-permute-start.2
  26.5 2.4 collective-permute-start.3
  30.2 1.8 collective-permute-done.3
  33.4 2.4 maximum_convert_fusion.1
  35.9 1.3 collective-permute-start.5
  37.2 6.5 collective-permute-start.4
  45.6 2.4 collective-permute-start.7
  47.9 3.5 collective-permute-start.6
  51.5 1.9 collective-permute-done.6
  55.6 2.2 copy-done.2
  57.8 2.5 maximum_convert_fusion
  60.6 55.4 %all-gather.5.cloned.1.call-done = bf16[32,256,128]{2,1,0:T(8,128)(2,1)} async-done(((bf16[8,256,128]{2,1,0:T(8,128)(2,1)}), bf16[32,256,128]{2,1,0:T(8,128)(2,1)}) %all-gather.5.cloned.1.call-update) | async-done | bytes 2097168 | tf_op jit(solution)/shard_map/all_gather | solution.py:65
  115.9 54.6 %while.55 = (s32[]{:T(128)}, f32[8,4,1024]{2,1,0:T(4,128)S(1)}, f32[8,4,1024]{2,1,0:T(4,128)}, f32[8,4,1024]{2,1,0:T(4,128)}, bf16[8,1024,128]{2,1,0:T(8,128)(2,...) while((s32[]{:T(128)}, f32[8,4,1024]{2,1,0:T(4,128)S(1)}, ...), condition=%wide.region_13.14_spmd.clone, body=%wide.region_0.13_spmd.clone.sunk | while | flops 137388160 | bytes 5588181 | solution.py:92
  117.2 1.2 fusion.187
  118.4 1.2 fusion.188
  119.6 1.2 fusion.189
  125.2 1.2 fusion.188
  126.5 1.2 fusion.189
  137.6 1.2 fusion.187
  138.9 1.2 fusion.188
  146.9 1.2 fusion.189
  158.1 1.2 fusion.187
  159.3 1.2 fusion.188
  160.6 1.2 fusion.189
  171.2 16.7 %all-gather = f32[32,4,1024]{2,1,0:T(4,128)S(1)} all-gather(f32[8,4,1024]{2,1,0:T(4,128)S(1)} %get-tuple-element.411), channel_id=2, replica_groups=mesh['lat'=16,'lon'=4,'bin'=4] {'bin'}, dimensions={0}, use_global_device_ids=true | all-gather | bytes 655360 | tf_op jit(solution)/shard_map/all_gather | solution.py:22
  187.8 16.7 %all-gather.1 = f32[32,4,1024]{2,1,0:T(4,128)S(1)} all-gather(f32[8,4,1024]{2,1,0:T(4,128)} %get-tuple-element.412), channel_id=3, replica_groups=mesh['lat'=16,'lon'=4,'bin'=4] {'bin'}, dimensions={0}, use_global_device_ids=true | all-gather | bytes 655360 | tf_op jit(solution)/shard_map/all_gather | solution.py:22
  204.5 16.5 %all-gather.2 = f32[32,4,1024]{2,1,0:T(4,128)S(1)} all-gather(f32[8,4,1024]{2,1,0:T(4,128)} %get-tuple-element.413), channel_id=4, replica_groups=mesh['lat'=16,'lon'=4,'bin'=4] {'bin'}, dimensions={0}, use_global_device_ids=true | all-gather | bytes 655360 | tf_op jit(solution)/shard_map/all_gather | solution.py:22
  221.8 3.5 while.54
  226.0 42.4 %while.56 = (s32[]{:T(128)}, f32[4,128,128]{2,1,0:T(8,128)S(1)}, f32[8,1024,128]{2,1,0:T(8,128)}, bf16[8,1024,128]{2,1,0:T(8,128)(2,1)S(1)}, bf16[4,128,128]{2,1...) while((s32[]{:T(128)}, f32[4,128,128]{2,1,0:T(8,128)S(1)}, ...), condition=%wide.region_19.20_spmd.clone, body=%wide.region_18.19_spmd.clone.sunk | while | flops 406257792 | bytes 9800433 | solution.py:116
  269.3 82.1 %reduce-scatter.2.cloned.1.call-done = f32[2048,128]{1,0:T(8,128)} async-done(((f32[8192,128]{1,0:T(8,128)}), f32[2048,128]{1,0:T(8,128)}) %reduce-scatter.2.cloned.1.call-update) | async-done | bytes 1048592 | tf_op jit(solution)/shard_map/reduce_scatter | solution.py:118
  351.4 1.4 select_convert_fusion
  352.8 1.3 collective-permute-start.9
  354.1 5.4 collective-permute-start.8
  359.5 4.6 fusion.126
  364.1 2.4 collective-permute-start.11
  366.6 3.4 collective-permute-start.10
  370.1 2.0 collective-permute-done.10
  374.2 2.2 copy-done.15
  376.4 8.8 fusion.101
  385.2 139.1 %psum.28 = f32[]{:T(128)} all-reduce(f32[]{:T(128)} %get-tuple-element.553), channel_id=1, replica_groups=mesh['lat'=16,'lon'=4,'bin'=4] {'lat','lon'}, use_global_device_ids=true, to_apply=%region_17.18 | all-reduce | flops 1 | bytes 8 | tf_op jit(solution)/shard_map/psum | solution.py:129
  525.0 335.9 %all-reduce.4.cloned.1.call-done = f32[4,128,128]{2,1,0:T(8,128)} async-done(((f32[4,128,128]{2,1,0:T(8,128)}), f32[4,128,128]{2,1,0:T(8,128)}) %all-reduce.4.cloned.1.call-update) | async-done | bytes 262160 | tf_op jit(solution)/shard_map/psum | solution.py:129
  860.9 266.5 %all-reduce.6.cloned.1.call-done = (f32[3,3,128,128]{3,2,1,0:T(8,128)}, f32[3,3,128,128]{3,2,1,0:T(8,128)}) async-done(((f32[3,3,128,128]{3,2,1,0:T(8,128)}, f32[3,3,128,128]{3,2,1,0:T(8,128)}), (f32[3,3,128,128]{3,2,1,0:T(8,128)}, f32[3,3,128,128]{3,2,1,0:T(8,128)})) %all-reduce.6.cloned.1.call-update) | async-done | bytes 1179664 | tf_op jit(solution)/shard_map/psum | solution.py:128
  1127.4 1.9 copy.85
  1129.3 1.9 copy.86
  1131.2 1.7 copy.87
  (286 shorter events, 100.4 us)
Async XLA Ops:
  7.2 26.2 %copy-start = (bf16[3,3,128,128]{3,2,1,0:T(8,128)(2,1)S(1)}, bf16[3,3,128,128]{3,2,1,0:T(8,128)(2,1)}, u32[]{:S(2)}) copy-start(bf16[3,3,128,128]{3,2,1,0:T(8,128)(2,1)} %param.20) | copy-start | bytes 884740
  7.2 25.3 %copy-start.5 = (bf16[8,256,128]{2,1,0:T(8,128)(2,1)S(1)}, bf16[8,256,128]{2,1,0:T(8,128)(2,1)}, u32[]{:S(2)}) copy-start(bf16[8,256,128]{2,1,0:T(8,128)(2,1)} %param.19) | copy-start | bytes 1572868
  7.2 108.7 %all-gather.5.cloned.1.call-start = ((), (), s32[]{:S(2)}) async-start(), calls=%async_computation.1 | async-start | bytes 2621440 | tf_op jit(solution)/shard_map/all_gather | solution.py:65
  8.2 7.1 collective-permute-start
  13.4 9.6 collective-permute-start.1
  23.0 5.9 collective-permute-start.2
  26.5 5.5 collective-permute-start.3
  33.4 18.1 %copy-start.6 = (bf16[8,256,1152]{2,1,0:T(8,128)(2,1)}, bf16[8,256,1152]{2,1,0:T(8,128)(2,1)S(1)}, u32[]{:S(2)}) copy-start(bf16[8,256,1152]{2,1,0:T(8,128)(2,1)S(1)} %fusion.110) | copy-start | bytes 14155780
  35.9 8.8 collective-permute-start.5
  37.2 8.4 collective-permute-start.4
  45.6 6.0 collective-permute-start.7
  47.9 5.5 collective-permute-start.6
  54.4 3.4 copy-start.11
  55.4 5.0 copy-start.14
  55.4 60.5 %copy-start.3 = (bf16[4,128,128]{2,1,0:T(8,128)(2,1)S(1)}, bf16[4,128,128]{2,1,0:T(8,128)(2,1)}, u32[]{:S(2)}) copy-start(bf16[4,128,128]{2,1,0:T(8,128)(2,1)} %param.22) | copy-start | bytes 393220
  55.6 2.2 copy-start.2
  60.3 291.1 %reduce-scatter.2.cloned.1.call-start = ((), (), s32[]{:S(2)}) async-start(), calls=%async_computation.2 | async-start | bytes 5242880 | tf_op jit(solution)/shard_map/reduce_scatter | solution.py:118
  170.5 0.7 copy-start.13
  171.2 54.8 %copy-start.1 = (bf16[8,1024,128]{2,1,0:T(8,128)(2,1)S(1)}, bf16[8,1024,128]{2,1,0:T(8,128)(2,1)}, u32[]{:S(2)}) copy-start(bf16[8,1024,128]{2,1,0:T(8,128)(2,1)} %get-tuple-element.944) | copy-start | bytes 6291460
  204.5 16.5 %copy-start.8 = (f32[32,4,1024]{2,1,0:T(4,128)}, f32[32,4,1024]{2,1,0:T(4,128)S(1)}, u32[]{:S(2)}) copy-start(f32[32,4,1024]{2,1,0:T(4,128)S(1)} %all-gather.1) | copy-start | bytes 1572868
  221.1 0.8 copy-start.9
  226.0 42.5 %copy-start.12 = (bf16[3,3,128,128]{3,2,1,0:T(8,128)(2,1)S(1)}, bf16[3,3,128,128]{3,2,1,0:T(8,128)(2,1)}, u32[]{:S(2)}) copy-start(bf16[3,3,128,128]{3,2,1,0:T(8,128)(2,1)} %param.21) | copy-start | bytes 884740
  268.5 0.7 copy-start.4
  268.5 82.9 %copy-start.7 = (f32[2048,128]{1,0:T(8,128)S(1)}, f32[2048,128]{1,0:T(8,128)}, u32[]{:S(2)}) copy-start(f32[2048,128]{1,0:T(8,128)} %get-tuple-element.613) | copy-start | bytes 3145732
  268.5 592.4 %all-reduce.4.cloned.1.call-start = ((), (), s32[]{:S(2)}) async-start(), calls=%async_computation.3 | async-start | bytes 524288 | tf_op jit(solution)/shard_map/psum | solution.py:129
  269.2 858.1 %all-reduce.6.cloned.1.call-start = ((), (), s32[]{:S(2)}) async-start(), calls=%async_computation.4 | async-start | bytes 2359296 | tf_op jit(solution)/shard_map/psum | solution.py:128
  352.8 11.3 collective-permute-start.9
  354.1 10.0 collective-permute-start.8
  364.1 5.9 collective-permute-start.11
  366.6 5.5 collective-permute-start.10
  373.1 3.3 copy-start.10
  374.2 2.2 copy-start.15
Sparse Core Ops, SparseCore 0:
  60.4 55.4 all-gather.4
  268.6 82.7 reduce-scatter.1
  354.8 506.0 all-reduce.3
  866.8 260.5 all-reduce.5
where the time goes:
time: 1140 us
  waiting for transfers between devices  755 us (66%)
  blocking collectives  189 us (17%)
  matrix products  92 us (8%)
  starting transfers between devices  38.7 us (3%)
  local copies, waits for them, and re-layouts  25.3 us (2%)
  other arithmetic  23.5 us (2%)
  between operations  16.2 us (1%)
    psum x1, waiting for transfers between devices, per_device(): head_grads, loss_sum = lax.psum((head_grads, loss_part), ('lat', 'lon'))  336 us
    psum x1, waiting for transfers between devices, per_device(): grad_one, grad_two = lax.psum((grad_one, grad_two), ('lat', 'lon', 'bin'))  267 us
    psum x1, blocking collectives, per_device(): head_grads, loss_sum = lax.psum((head_grads, loss_part), ('lat', 'lon'))  139 us
    reduce_scatter x1, waiting for transfers between devices, per_device(): lax.psum_scatter(hidden_back, 'bin', scatter_dimension=0, tiled=True)  82.1 us
    all_gather x1, waiting for transfers between devices, per_device(): lax.all_gather(act_two.reshape(grid_rows, grid_cols, channels), 'bin', ax...  55.4 us
    all_gather x3, blocking collectives, merged(): everything = jax.tree.map(lambda part: lax.all_gather(part, axis), shard)  49.9 us
    dot_general x32, matrix products, head_stats(): jnp.dot(feat_rows, head_weight[k], preferred_element_type=jnp.float32)  39.3 us
    ppermute x6, starting transfers between devices, extended(): before = lax.ppermute(last, axis, up)  27.5 us
  transfers between devices with their start and end apart: 16, of which 11 were waited for; matrix products, arithmetic and copies ran while one was open for 2% of the time, Pallas kernels for 0%

commit v1 on v0

--- a/solution.py
+++ b/solution.py
@@ -125,7 +125,7 @@
     back_act = jnp.dot(outer_two, flipped, preferred_element_type=jnp.float32)
     back_one = jnp.where(pre_one > 0, back_act, 0.0).astype(jnp.bfloat16)
     grad_one = jnp.einsum("nk,nc->kc", inner_one, back_one, preferred_element_type=jnp.float32)
-    grad_one, grad_two = lax.psum((grad_one, grad_two), ("lat", "lon", "bin"))
+    grad_one, grad_two = lax.psum(lax.psum((grad_one, grad_two), ("lon", "bin")), "lat")
     head_grads, loss_sum = lax.psum((head_grads, loss_part), ("lat", "lon"))
     loss_mean = loss_sum / (head_count * cells_all)
     grad_conv_one = grad_one.reshape(3, 3, channels, channels)

time: 1140 us -> 1210 us (1.061)
  waiting for transfers between devices: 755 us -> 819 us
    psum x1, waiting for transfers between devices: 336 us -> 368 us  [per_device(): head_grads, loss_sum = lax.psum((head_grads, loss_part), ('lat', 'lon'))]
    psum x1 -> x2, waiting for transfers between devices: 267 us -> 297 us  [the longest x1 168 us: per_device(): lax.psum((grad_one, grad_two), ('lon', 'bin'))]
  transfers between devices with their start and end apart: 16 -> 17, of which waited for: 11 -> 12; matrix products, arithmetic and copies ran while one was open for 2% -> 1% of each run, Pallas kernels for 0% -> 0%
where the time goes in v1:
time: 1210 us
  waiting for transfers between devices  819 us (68%)
  blocking collectives  194 us (16%)
  matrix products  92.1 us (8%)
  starting transfers between devices  38.7 us (3%)
  local copies, waits for them, and re-layouts  24.9 us (2%)
  other arithmetic  23.5 us (2%)
  between operations  16.2 us (1%)
    psum x1, waiting for transfers between devices, per_device(): head_grads, loss_sum = lax.psum((head_grads, loss_part), ('lat', 'lon'))  368 us
    psum x1, waiting for transfers between devices, per_device(): lax.psum((grad_one, grad_two), ('lon', 'bin'))  168 us
    psum x1, blocking collectives, per_device(): head_grads, loss_sum = lax.psum((head_grads, loss_part), ('lat', 'lon'))  144 us
    psum x1, waiting for transfers between devices, per_device(): lax.psum(lax.psum((grad_one, grad_two), ('lon', 'bin')), 'lat')  129 us
    reduce_scatter x1, waiting for transfers between devices, per_device(): lax.psum_scatter(hidden_back, 'bin', scatter_dimension=0, tiled=True)  83.2 us
    all_gather x1, waiting for transfers between devices, per_device(): lax.all_gather(act_two.reshape(grid_rows, grid_cols, channels), 'bin', ax...  55.4 us
    all_gather x3, blocking collectives, merged(): everything = jax.tree.map(lambda part: lax.all_gather(part, axis), shard)  49.3 us
    dot_general x32, matrix products, head_stats(): jnp.dot(feat_rows, head_weight[k], preferred_element_type=jnp.float32)  39.3 us
  transfers between devices with their start and end apart: 17, of which 12 were waited for; matrix products, arithmetic and copies ran while one was open for 1% of the time, Pallas kernels for 0%

profile of v1, /device:TPU:8, one launch (start us, length us, event | category | flops | bytes accessed | tf_op | source)
XLA Modules:
  0.0 1208.9 jit_solution(14192364226053998317)
XLA Ops:
  8.2 5.2 collective-permute-start
  13.4 1.3 collective-permute-start.1
  16.4 6.6 collective-permute-done.1
  23.0 3.5 collective-permute-start.2
  26.5 2.4 collective-permute-start.3
  30.2 1.8 collective-permute-done.3
  33.4 2.5 maximum_convert_fusion.1
  35.9 1.3 collective-permute-start.5
  37.2 6.5 collective-permute-start.4
  45.6 2.4 collective-permute-start.7
  47.9 3.5 collective-permute-start.6
  51.5 1.9 collective-permute-done.6
  55.6 2.2 copy-done.2
  57.8 2.5 maximum_convert_fusion
  60.6 55.4 %all-gather.5.cloned.1.call-done = bf16[32,256,128]{2,1,0:T(8,128)(2,1)} async-done(((bf16[8,256,128]{2,1,0:T(8,128)(2,1)}), bf16[32,256,128]{2,1,0:T(8,128)(2,1)}) %all-gather.5.cloned.1.call-update) | async-done | bytes 2097168 | tf_op jit(solution)/shard_map/all_gather | solution.py:65
  115.9 54.6 %while.55 = (s32[]{:T(128)}, f32[8,4,1024]{2,1,0:T(4,128)S(1)}, f32[8,4,1024]{2,1,0:T(4,128)}, f32[8,4,1024]{2,1,0:T(4,128)}, bf16[8,1024,128]{2,1,0:T(8,128)(2,...) while((s32[]{:T(128)}, f32[8,4,1024]{2,1,0:T(4,128)S(1)}, ...), condition=%wide.region_13.14_spmd.clone, body=%wide.region_0.13_spmd.clone.sunk | while | flops 137388160 | bytes 5588181 | solution.py:92
  117.2 1.2 fusion.187
  118.4 1.2 fusion.188
  119.6 1.2 fusion.189
  125.2 1.2 fusion.188
  126.5 1.2 fusion.189
  137.6 1.2 fusion.187
  138.9 1.2 fusion.188
  146.9 1.2 fusion.189
  158.1 1.2 fusion.187
  159.3 1.2 fusion.188
  171.2 16.7 %all-gather = f32[32,4,1024]{2,1,0:T(4,128)S(1)} all-gather(f32[8,4,1024]{2,1,0:T(4,128)S(1)} %get-tuple-element.411), channel_id=2, replica_groups=mesh['lat'=16,'lon'=4,'bin'=4] {'bin'}, dimensions={0}, use_global_device_ids=true | all-gather | bytes 655360 | tf_op jit(solution)/shard_map/all_gather | solution.py:22
  187.8 16.8 %all-gather.1 = f32[32,4,1024]{2,1,0:T(4,128)S(1)} all-gather(f32[8,4,1024]{2,1,0:T(4,128)} %get-tuple-element.412), channel_id=3, replica_groups=mesh['lat'=16,'lon'=4,'bin'=4] {'bin'}, dimensions={0}, use_global_device_ids=true | all-gather | bytes 655360 | tf_op jit(solution)/shard_map/all_gather | solution.py:22
  204.7 15.9 %all-gather.2 = f32[32,4,1024]{2,1,0:T(4,128)S(1)} all-gather(f32[8,4,1024]{2,1,0:T(4,128)} %get-tuple-element.413), channel_id=4, replica_groups=mesh['lat'=16,'lon'=4,'bin'=4] {'bin'}, dimensions={0}, use_global_device_ids=true | all-gather | bytes 655360 | tf_op jit(solution)/shard_map/all_gather | solution.py:22
  221.3 3.5 while.54
  225.5 42.5 %while.56 = (s32[]{:T(128)}, f32[4,128,128]{2,1,0:T(8,128)S(1)}, f32[8,1024,128]{2,1,0:T(8,128)}, bf16[8,1024,128]{2,1,0:T(8,128)(2,1)S(1)}, bf16[4,128,128]{2,1...) while((s32[]{:T(128)}, f32[4,128,128]{2,1,0:T(8,128)S(1)}, ...), condition=%wide.region_19.20_spmd.clone, body=%wide.region_18.19_spmd.clone.sunk | while | flops 406257792 | bytes 9800433 | solution.py:116
  268.3 83.2 %reduce-scatter.2.cloned.1.call-done = f32[2048,128]{1,0:T(8,128)} async-done(((f32[8192,128]{1,0:T(8,128)}), f32[2048,128]{1,0:T(8,128)}) %reduce-scatter.2.cloned.1.call-update) | async-done | bytes 1048592 | tf_op jit(solution)/shard_map/reduce_scatter | solution.py:118
  351.5 1.4 select_convert_fusion
  352.9 1.3 collective-permute-start.9
  354.2 5.4 collective-permute-start.8
  359.6 4.6 fusion.126
  364.3 2.4 collective-permute-start.11
  366.7 3.5 collective-permute-start.10
  370.2 2.0 collective-permute-done.10
  374.3 2.2 copy-done.15
  376.5 8.8 fusion.101
  385.9 167.7 %all-reduce.8.cloned.1.call-done = (f32[1152,128]{1,0:T(8,128)}, f32[1152,128]{1,0:T(8,128)}) async-done(((f32[1152,128]{1,0:T(8,128)}, f32[1152,128]{1,0:T(8,128)}), (f32[1152,128]{1,0:T(8,128)}, f32[1152,128]{1,0:T(8,128)})) %all-reduce.8.cloned.1.call-update) | async-done | bytes 1179664 | tf_op jit(solution)/shard_map/psum | solution.py:128
  553.7 144.3 %psum.42 = f32[]{:T(128)} all-reduce(f32[]{:T(128)} %get-tuple-element.555), channel_id=1, replica_groups=mesh['lat'=16,'lon'=4,'bin'=4] {'lat','lon'}, use_global_device_ids=true, to_apply=%region_17.18 | all-reduce | flops 1 | bytes 8 | tf_op jit(solution)/shard_map/psum | solution.py:129
  698.7 367.8 %all-reduce.6.cloned.1.call-done = f32[4,128,128]{2,1,0:T(8,128)} async-done(((f32[4,128,128]{2,1,0:T(8,128)}), f32[4,128,128]{2,1,0:T(8,128)}) %all-reduce.6.cloned.1.call-update) | async-done | bytes 262160 | tf_op jit(solution)/shard_map/psum | solution.py:129
  1066.5 129.2 %all-reduce.10.cloned.1.call-done = (f32[3,3,128,128]{3,2,1,0:T(8,128)}, f32[3,3,128,128]{3,2,1,0:T(8,128)}) async-done(((f32[3,3,128,128]{3,2,1,0:T(8,128)}, f32[3,3,128,128]{3,2,1,0:T(8,128)}), (f32[3,3,128,128]{3,2,1,0:T(8,128)}, f32[3,3,128,128]{3,2,1,0:T(8,128)})) %all-reduce.10.cloned.1.call-update) | async-done | bytes 1179664 | tf_op jit(solution)/shard_map/psum | solution.py:128
  1195.7 1.9 copy.87
  1197.6 1.9 copy.88
  1199.5 1.7 copy.89
  (289 shorter events, 101.9 us)
Async XLA Ops:
  7.2 26.2 %copy-start = (bf16[3,3,128,128]{3,2,1,0:T(8,128)(2,1)S(1)}, bf16[3,3,128,128]{3,2,1,0:T(8,128)(2,1)}, u32[]{:S(2)}) copy-start(bf16[3,3,128,128]{3,2,1,0:T(8,128)(2,1)} %param.20) | copy-start | bytes 884740
  7.2 25.3 %copy-start.5 = (bf16[8,256,128]{2,1,0:T(8,128)(2,1)S(1)}, bf16[8,256,128]{2,1,0:T(8,128)(2,1)}, u32[]{:S(2)}) copy-start(bf16[8,256,128]{2,1,0:T(8,128)(2,1)} %param.19) | copy-start | bytes 1572868
  7.2 108.7 %all-gather.5.cloned.1.call-start = ((), (), s32[]{:S(2)}) async-start(), calls=%async_computation.1 | async-start | bytes 2621440 | tf_op jit(solution)/shard_map/all_gather | solution.py:65
  8.2 7.1 collective-permute-start
  13.4 9.6 collective-permute-start.1
  23.0 5.9 collective-permute-start.2
  26.5 5.5 collective-permute-start.3
  33.4 18.1 %copy-start.6 = (bf16[8,256,1152]{2,1,0:T(8,128)(2,1)}, bf16[8,256,1152]{2,1,0:T(8,128)(2,1)S(1)}, u32[]{:S(2)}) copy-start(bf16[8,256,1152]{2,1,0:T(8,128)(2,1)S(1)} %fusion.110) | copy-start | bytes 14155780
  35.9 8.8 collective-permute-start.5
  37.2 8.4 collective-permute-start.4
  45.6 6.0 collective-permute-start.7
  47.9 5.5 collective-permute-start.6
  54.4 3.4 copy-start.11
  55.4 5.0 copy-start.14
  55.4 60.5 %copy-start.3 = (bf16[4,128,128]{2,1,0:T(8,128)(2,1)S(1)}, bf16[4,128,128]{2,1,0:T(8,128)(2,1)}, u32[]{:S(2)}) copy-start(bf16[4,128,128]{2,1,0:T(8,128)(2,1)} %param.22) | copy-start | bytes 393220
  55.6 2.2 copy-start.2
  60.3 291.2 %reduce-scatter.2.cloned.1.call-start = ((), (), s32[]{:S(2)}) async-start(), calls=%async_computation.2 | async-start | bytes 5242880 | tf_op jit(solution)/shard_map/reduce_scatter | solution.py:118
  170.5 0.7 copy-start.13
  171.2 54.3 %copy-start.1 = (bf16[8,1024,128]{2,1,0:T(8,128)(2,1)S(1)}, bf16[8,1024,128]{2,1,0:T(8,128)(2,1)}, u32[]{:S(2)}) copy-start(bf16[8,1024,128]{2,1,0:T(8,128)(2,1)} %get-tuple-element.950) | copy-start | bytes 6291460
  204.7 15.9 %copy-start.8 = (f32[32,4,1024]{2,1,0:T(4,128)}, f32[32,4,1024]{2,1,0:T(4,128)S(1)}, u32[]{:S(2)}) copy-start(f32[32,4,1024]{2,1,0:T(4,128)S(1)} %all-gather.1) | copy-start | bytes 1572868
  220.5 0.8 copy-start.9
  225.5 42.6 %copy-start.12 = (bf16[3,3,128,128]{3,2,1,0:T(8,128)(2,1)S(1)}, bf16[3,3,128,128]{3,2,1,0:T(8,128)(2,1)}, u32[]{:S(2)}) copy-start(bf16[3,3,128,128]{3,2,1,0:T(8,128)(2,1)} %param.21) | copy-start | bytes 884740
  268.0 96.2 %copy-start.4 = (f32[4,128,128]{2,1,0:T(8,128)}, f32[4,128,128]{2,1,0:T(8,128)S(1)}, u32[]{:S(2)}) copy-start(f32[4,128,128]{2,1,0:T(8,128)S(1)} %get-tuple-element.418) | copy-start | bytes 786436
  268.0 83.5 %copy-start.7 = (f32[2048,128]{1,0:T(8,128)S(1)}, f32[2048,128]{1,0:T(8,128)}, u32[]{:S(2)}) copy-start(f32[2048,128]{1,0:T(8,128)} %get-tuple-element.615) | copy-start | bytes 3145732
  268.0 285.6 %all-reduce.8.cloned.1.call-start = ((), (), s32[]{:S(2)}) async-start(), calls=%async_computation.4 | async-start | bytes 2359296 | tf_op jit(solution)/shard_map/psum | solution.py:128
  352.9 11.3 collective-permute-start.9
  354.2 10.1 collective-permute-start.8
  364.3 5.9 collective-permute-start.11
  366.7 5.5 collective-permute-start.10
  373.2 3.3 copy-start.10
  374.3 2.2 copy-start.15
  385.3 681.2 %all-reduce.6.cloned.1.call-start = ((), (), s32[]{:S(2)}) async-start(), calls=%async_computation.3 | async-start | bytes 524288 | tf_op jit(solution)/shard_map/psum | solution.py:129
  385.9 809.9 %all-reduce.10.cloned.1.call-start = ((), (), s32[]{:S(2)}) async-start(), calls=%async_computation.5 | async-start | bytes 2359296 | tf_op jit(solution)/shard_map/psum | solution.py:128
Sparse Core Ops, SparseCore 0:
  60.4 55.4 all-gather.4
  268.2 83.3 reduce-scatter.1
  385.4 168.1 all-reduce.7
  556.9 509.5 all-reduce.5
  1069.0 126.6 all-reduce.9
